TPU v7x, 32 devices: a whole 2x2x4 slice. The times are simulated.
32 devices in a mesh: chan: 8 (over z, y), facet: 4 (over x, core).
Axes of the slice: x: 2, y: 2, z: 4, core: 2. Of those that a mesh axis runs over, the one named last changes fastest.
Arguments:
- solution: float32 [8, 2048, 2048], P('chan', 'facet'), may hold values from -6 to 6
- residual: float32 [8, 2048, 2048], P('chan', 'facet'), may hold values from -120 to 120
- direction: float32 [8, 2048, 2048], P('chan', 'facet'), may hold values from -120 to 120
- spectra: float32 [8, 4096, 4096], P('chan', None, 'facet'), may hold values from 0.05 to 1
- basis: float32 [8, 8], replicated, may hold values from -2 to 2
- slot_channel: int32 [8], replicated, may hold values from 0 to 7, each once
Outputs:
- new_solution: float32 [8, 2048, 2048], P('chan', 'facet')
- new_residual: float32 [8, 2048, 2048], P('chan', 'facet')
- new_direction: float32 [8, 2048, 2048], P('chan', 'facet')
Inputs may be any that keep to these rules, and one draw needn't show every extreme that they name: `slot_channel`: every channel appears in exactly one slot.
All inputs are finite; a program needn't handle non-finite values.
Results may differ from a plain program's by a relative error of at most 0.000064.
Values sent between devices are 32-bit elements; how exact they have to be, the bound alone decides.
A program may use at most 256 MiB of HBM per device.

v0:
```python
import math
import jax
import jax.numpy as jnp
from jax import lax
from jax.sharding import PartitionSpec as P

ROOT = 64
HIGH = lax.Precision.HIGH
HIGHEST = lax.Precision.HIGHEST
PRIOR_FLOOR = 0.25


def wave(product, length, direction_sign):
    angles = (product % length).astype(jnp.float32) * (2.0 * math.pi / length)
    return (jnp.cos(angles), direction_sign * jnp.sin(angles))


def span(size):
    return jnp.arange(size, dtype=jnp.int32)


def swap_pairs(array, count, bit):
    pairs = [(place, place ^ bit) for place in range(count)]
    return lax.ppermute(array, "facet", pairs)


def column_table(width, columns, length, first_column):
    column = first_column + span(columns)[None, :]
    coarse = width // ROOT
    coarse_real, coarse_imag = wave(span(coarse)[:, None] * ROOT * column, length, -1.0)
    fine_real, fine_imag = wave(span(ROOT)[:, None] * column, length, -1.0)
    coarse_real, coarse_imag = (coarse_real[:, None], coarse_imag[:, None])
    fine_real, fine_imag = (fine_real[None], fine_imag[None])
    table_real = (coarse_real * fine_real - coarse_imag * fine_imag).reshape(width, columns)
    table_imag = (coarse_real * fine_imag + coarse_imag * fine_real).reshape(width, columns)
    return lax.optimization_barrier((table_real, table_imag))


def complex_stack(real, imag):
    return jnp.stack([jnp.stack([real, imag]), jnp.stack([-imag, real])])


def row_spectrum_pass(planes, spectrum, row_digits, factor):
    halved, columns = (row_digits.shape[0], planes.shape[2])
    blocks = planes.reshape(2, halved, factor, columns)
    first = complex_stack(*wave(row_digits[:, None] * span(factor)[None, :], factor, -1.0))
    section = jnp.einsum("pjnc,pqjk->kqnc", blocks, first, precision=HIGH)
    spread = (
        span(factor)[:, None, None] * span(factor)[None, :, None]
        + span(factor)[None, :, None] * span(factor)[None, None, :] * factor
    )
    second = complex_stack(*wave(spread, factor * factor, -1.0))
    freqs = jnp.einsum("kpnc,pqknj->kqjc", section, second, precision=HIGH)
    spectrum = spectrum.reshape(factor, factor, columns).transpose(1, 0, 2)
    weighted = freqs * spectrum[:, None]
    third = complex_stack(*wave(spread, factor * factor, 1.0))
    section = jnp.einsum("kpjc,pqknj->kqnc", weighted, third, precision=HIGH)
    last = complex_stack(*wave(row_digits[:, None] * span(factor)[None, :], factor, 1.0))
    rows = jnp.einsum("kpnc,pqjk->qjnc", section, last, precision=HIGH)
    return rows.reshape(2, halved * factor, columns)


def body(solution, residual, direction, spectra, basis, slot_channel):
    channel_count = basis.shape[0]
    factor = ROOT
    length = factor * factor
    facets = lax.axis_size("facet")
    place = lax.axis_index("facet")
    height, width = direction.shape[1:]
    columns = spectra.shape[2]
    own = direction[0]
    blocks = {0: own}
    bit = facets // 2
    while bit:
        blocks.update({key ^ bit: swap_pairs(blocks[key], facets, bit) for key in list(blocks)})
        bit //= 2
    table_real, table_imag = column_table(width, columns, length, place * columns)
    near = [blocks[key] for key in range(facets // 2)]
    far = [blocks[key] for key in range(facets // 2, facets)]
    near_rows = jnp.concatenate(near, axis=0)
    far_rows = jnp.concatenate(far, axis=0)
    planes = jnp.stack(
        [
            jnp.concatenate(
                [jnp.dot(part, table, precision=HIGH) for part in (near_rows, far_rows)], axis=0
            )
            for table in (table_real, table_imag)
        ]
    )
    digits = height // factor
    row_digits = ((place ^ span(facets))[:, None] * digits + span(digits)[None, :]).reshape(-1)
    rows = row_spectrum_pass(planes, spectra[0], row_digits, factor)

    def partial(part):
        wide = (((1,), (1,)), ((), ()))
        return lax.dot_general(part[0], table_real, wide, precision=HIGH) + lax.dot_general(
            part[1], table_imag, wide, precision=HIGH
        )

    sums = {}
    half = facets // 2
    for base in (half, 0):
        image = partial(rows[:, base * height : (base + half) * height])
        for key in range(half):
            sums[base + key] = image[key * height : (key + 1) * height]
    bit = 1
    while bit < facets:
        sums = {
            key: sums[key] + swap_pairs(sums[key | bit], facets, bit)
            for key in sorted(sums, reverse=True)
            if not key & bit
        }
        bit *= 2
    blurred = sums[0][None] * (1.0 / float(length * length))
    regrouped = lax.all_to_all(direction, "chan", split_axis=1, concat_axis=0, tiled=True)
    one_hot = (slot_channel[:, None] == span(channel_count)[None, :]).astype(jnp.float32)
    loadings = jnp.dot(one_hot, basis, precision=HIGHEST)
    coeffs = jnp.einsum("cq,cij->qij", loadings, regrouped, precision=HIGHEST)
    local_prior = PRIOR_FLOOR * regrouped + jnp.einsum(
        "cq,qij->cij", loadings, coeffs, precision=HIGHEST
    )
    prior_term = lax.all_to_all(local_prior, "chan", split_axis=0, concat_axis=1, tiled=True)
    applied = blurred + prior_term
    moments = jnp.stack(
        [
            jnp.sum(residual * residual),
            jnp.sum(direction * applied),
            jnp.sum(residual * applied),
            jnp.sum(applied * applied),
        ]
    )
    norm_now, curvature, cross, square = lax.psum(moments, ("chan", "facet"))
    step_size = norm_now / curvature
    new_solution = solution + step_size * direction
    new_residual = residual - step_size * applied
    norm_next = norm_now - 2.0 * step_size * cross + step_size * step_size * square
    new_direction = new_residual + norm_next / norm_now * direction
    return (new_solution, new_residual, new_direction)


def solution(mesh):
    return jax.shard_map(
        body,
        mesh=mesh,
        in_specs=(
            P("chan", "facet", None),
            P("chan", "facet", None),
            P("chan", "facet", None),
            P("chan", None, "facet"),
            P(),
            P(),
        ),
        out_specs=(P("chan", "facet", None), P("chan", "facet", None), P("chan", "facet", None)),
        check_vma=False,
    )
```

profile of v0, /device:TPU:0, one launch (start us, length us, event | category | flops | bytes accessed | tf_op | source)
XLA Modules:
  0.0 682.2 jit_solution(11598784250257221795)
XLA Ops:
  3.7 8.5 %copy.27 = f32[1,512,2048]{2,0,1:T(1,128)} copy(f32[1,512,2048]{2,1,0:T(8,128)} %param.8) | data formatting | bytes 8388608 | tf_op args[2]
  27.4 67.2 %collective-permute-done.1 = f32[512,2048]{1,0:T(8,128)} collective-permute-done((f32[512,2048]{1,0:T(8,128)}, f32[512,2048]{1,0:T(8,128)}, u32[]{:S(2)}, u32[]{:S(2)}) %collective-permute-start.1) | collective-permute-done | bytes 4194336 | tf_op jit(solution)/shard_map/ppermute | solution.py:24
  94.7 17.8 %copy.73 = f32[64,64,1024]{2,0,1:T(8,128)} copy(f32[64,64,1024]{2,1,0:T(8,128)} %bitcast.135) | data formatting | bytes 33554432 | tf_op jit(solution)/shard_map/reshape;squeeze | solution.py:54
  112.4 9.1 %fusion.41 = (f32[1,64,64,64]{2,3,1,0:T(8,128)S(1)}, f32[1,64,64,64]{2,3,1,0:T(8,128)S(1)}, f32[1,64,64,64]{2,3,1,0:T(8,128)S(1)}, f32[1,64,64,64]{2,3,1,0:T(8,128)S(1)}, f32[1,64,64,64]{2,3,1,0:T(8,128)}) fusion(s32[64,64]{0,1:T(8,128)S(1)} %broadcast_multiply_fusion.1, s32[64,64]{1,0:T(8,128)S(1)} %copy.17), kind=kLoop, calls=%fused_computation.73 | loop fusion | flops 4456448 | bytes 5275648 | tf_op jit(solution)/shard_map/sin | solution.py:15
  138.1 18.5 %fusion.17 = f32[1024,1024]{1,0:T(8,128)} fusion(f32[2048,1024]{1,0:T(8,128)} %bitcast.142, f32[512,2048]{1,0:T(8,128)} %collective-permute-done, f32[512,2048]{1,0:T(8,128)S(1)} %bitcast.129), kind=kOutput, calls=%fused_computation.26 | convolution fusion | flops 12886999040 | bytes 20971520 | tf_op jit(solution)/shard_map/dot_general | solution.py:85
  156.6 14.4 %fusion.16 = f32[1024,1024]{1,0:T(8,128)S(1)} fusion(f32[2048,1024]{1,0:T(8,128)S(1)} %bitcast.152, f32[512,2048]{1,0:T(8,128)} %collective-permute-done, f32[512,2048]{1,0:T(8,128)S(1)} %bitcast.130), kind=kOutput, calls=%fused_computation.25 | convolution fusion | flops 12886999040 | bytes 20971520 | tf_op jit(solution)/shard_map/dot_general | solution.py:85
  175.7 17.8 %fusion.79 = f32[1024,1024]{1,0:T(8,128)} fusion(f32[1024,2048]{1,0:T(8,128)} %constant_dynamic-update-slice_fusion, f32[2048,1024]{1,0:T(8,128)S(1)} %bitcast.147), kind=kOutput, calls=%fused_computation.140 | convolution fusion | flops 12884901888 | bytes 20971520 | tf_op jit(solution)/shard_map/dot_general | solution.py:85
  193.6 17.6 %fusion.80 = f32[1024,1024]{1,0:T(8,128)} fusion(f32[1024,2048]{1,0:T(8,128)} %constant_dynamic-update-slice_fusion, f32[2048,1024]{1,0:T(8,128)S(1)} %bitcast.153), kind=kOutput, calls=%fused_computation.141 | convolution fusion | flops 12884901888 | bytes 20971520 | tf_op jit(solution)/shard_map/dot_general | solution.py:85
  215.5 8.1 %copy.19 = f32[1,32,64,1024]{3,1,0,2:T(8,128)} copy(f32[1,32,64,1024]{3,2,1,0:T(8,128)S(1)} %bitcast.133) | data formatting | bytes 16777216 | tf_op jit(solution)/shard_map/stack | solution.py:82
  226.9 8.1 %copy.20 = f32[1,32,64,1024]{3,1,0,2:T(8,128)} copy(f32[1,32,64,1024]{3,2,1,0:T(8,128)S(1)} %bitcast.134) | data formatting | bytes 16777216 | tf_op jit(solution)/shard_map/stack | solution.py:82
  235.4 27.6 %convolution_bitcast_fusion = f32[64,2,64,1024,1]{3,0,2,1,4:T(8,128)} fusion(f32[1,32,64,1024]{3,1,0,2:T(8,128)} %copy.20, f32[1,32,64,1024]{3,1,0,2:T(8,128)} %copy.19, f32[1,2,32,64]{3,2,0,1:T(8,128)S(1)} %get-tuple-element.26, f32[1,2,32,64]{3,2,0,1:T(8,128)S(1)} %get-tuple-element.27), kind=kOutput, calls=%fused_computation.9 | convolution fusion | flops 3225427968 | bytes 50364416 | tf_op jit(solution)/shard_map/pjnc,pqjk->kqnc/dot_general | solution.py:47
  263.0 47.3 %fusion.4 = f32[64,2,64,1024,1]{3,2,1,0,4:T(8,128)} fusion(f32[64,2,64,1024,1]{3,0,2,1,4:T(8,128)} %convolution_bitcast_fusion, f32[2,2,64,64,64]{3,4,2,1,0:T(8,128)} %get-tuple-element.43), kind=kOutput, calls=%fused_computation.5 | convolution fusion | flops 6442450944 | bytes 71303168 | tf_op jit(solution)/shard_map/kpnc,pqknj->kqjc/dot_general | solution.py:53
  310.3 31.7 %fusion.11 = f32[64,2,64,1024]{3,2,1,0:T(8,128)} fusion(f32[64,2,64,1024,1]{3,2,1,0,4:T(8,128)} %fusion.4, f32[64,64,1024]{2,1,0:T(8,128)} %bitcast.126, f32[2,2,64,64,64]{3,4,2,1,0:T(8,128)} %get-tuple-element.42), kind=kOutput, calls=%fused_computation.15 | convolution fusion | flops 6450839552 | bytes 88080384 | tf_op jit(solution)/shard_map/kpjc,pqknj->kqnc/dot_general | solution.py:57
  342.0 40.1 %fusion.18 = f32[2,32,64,1024]{3,1,2,0:T(8,128)S(1)} fusion(f32[64,2,64,1024]{3,2,1,0:T(8,128)} %fusion.11, f32[1,2,32,64]{3,2,1,0:T(8,128)S(1)} %get-tuple-element.28, f32[1,2,32,64]{3,2,1,0:T(8,128)S(1)} %get-tuple-element.25), kind=kOutput, calls=%fused_computation.27 | convolution fusion | flops 3221233664 | bytes 50364416 | tf_op jit(solution)/shard_map/kpnc,pqjk->qjnc/dot_general | solution.py:59
  382.2 19.4 %copy.26 = f32[2,32,64,1024]{3,2,1,0:T(8,128)} copy(f32[2,32,64,1024]{3,1,2,0:T(8,128)S(1)} %fusion.18) | data formatting | bytes 33554432 | tf_op jit(solution)/shard_map/kpnc,pqjk->qjnc/dot_general | solution.py:59
  401.6 16.8 %fusion.25 = f32[1024,2048]{1,0:T(8,128)S(1)} fusion(f32[2048,1024]{1,0:T(8,128)} %bitcast.148, f32[2,2048,1024]{2,1,0:T(8,128)} %bitcast.136), kind=kOutput, calls=%fused_computation.38 | convolution fusion | flops 12884901888 | bytes 20971520 | tf_op jit(solution)/shard_map/dot_general | solution.py:96
  418.4 18.0 %fusion.37 = f32[1024,2048]{1,0:T(8,128)S(1)} fusion(f32[1024,2048]{1,0:T(8,128)S(1)} %fusion.25, f32[2048,1024]{1,0:T(8,128)} %bitcast.143, f32[2,2048,1024]{2,1,0:T(8,128)} %bitcast.137), kind=kOutput, calls=%fused_computation.65 | convolution fusion | flops 12886999040 | bytes 29360128 | tf_op jit(solution)/shard_map/dot_general | solution.py:96
  468.8 18.3 %fusion.30 = f32[1024,2048]{1,0:T(8,128)} fusion(f32[2048,1024]{1,0:T(8,128)} %bitcast.149, f32[2,2048,1024]{2,1,0:T(8,128)} %bitcast.138), kind=kOutput, calls=%fused_computation.46 | convolution fusion | flops 12884901888 | bytes 20971520 | tf_op jit(solution)/shard_map/dot_general | solution.py:96
  487.2 18.1 %fusion.36 = f32[1024,2048]{1,0:T(8,128)S(1)} fusion(f32[1024,2048]{1,0:T(8,128)} %fusion.30, f32[2048,1024]{1,0:T(8,128)} %bitcast.144, f32[2,2048,1024]{2,1,0:T(8,128)} %bitcast.139), kind=kOutput, calls=%fused_computation.64 | convolution fusion | flops 12886999040 | bytes 29360128 | tf_op jit(solution)/shard_map/dot_general | solution.py:96
  515.8 46.5 %all-to-all-done.1 = f32[8,64,2048]{2,1,0:T(8,128)} async-done(((f32[8,64,2048]{2,1,0:T(8,128)}), f32[8,64,2048]{2,1,0:T(8,128)}, u32[]{:S(2)}, u32[]{:S(2)}) %all-to-all-start.1) | async-done | bytes 4194336 | tf_op jit(solution)/shard_map/all_to_all | solution.py:122
  562.3 44.5 %collective-permute-done.5 = f32[512,2048]{1,0:T(8,128)} collective-permute-done((f32[512,2048]{1,0:T(8,128)}, f32[512,2048]{1,0:T(8,128)}, u32[]{:S(2)}, u32[]{:S(2)}) %collective-permute-start.5) | collective-permute-done | bytes 4194336 | tf_op jit(solution)/shard_map/ppermute | solution.py:24
  606.8 10.3 %multiply_reduce_fusion.1 = (f32[]{:T(128)}, f32[]{:T(128)}, f32[]{:T(128)}, f32[512,2048]{1,0:T(8,128)S(1)}) fusion(f32[1,512,2048]{2,1,0:T(8,128)} %param.7, f32[1,512,2048]{2,1,0:T(8,128)} %param.8, f32[8,64,2048]{2,1,0:T(8,128)} %all-to-all-done.1, f32[512,2048]{1,0:T(8,128)} %collective-permute-done.5, f32[512,2048]{1,0:T(8,128)} %collective-permute-done.3, ...), kind=kLoop, calls=%fused_computation.58 | loop fusion | flops 10485757 | bytes 29360140 | tf_op jit(solution)/shard_map/reduce_sum | solution.py:126
  623.5 40.9 %psum.7 = f32[4]{0:T(128)S(1)} all-reduce(f32[4]{0:T(128)S(1)} %pad_maximum_fusion.15), channel_id=1, replica_groups=mesh['chan'=8,'facet'=4] {'chan','facet'}, use_global_device_ids=true, to_apply=%region_4.5 | all-reduce | flops 4 | bytes 32 | tf_op jit(solution)/shard_map/psum | solution.py:132
  669.1 12.8 %multiply_add_fusion.1 = (f32[1,512,2048]{2,1,0:T(8,128)}, f32[1,512,2048]{2,1,0:T(8,128)}, f32[1,512,2048]{2,1,0:T(8,128)}) fusion(f32[1,512,2048]{2,1,0:T(8,128)} %param.8, f32[]{:T(128)S(6)} %div.7, f32[1,512,2048]{2,1,0:T(8,128)} %param.7, f32[512,2048]{1,0:T(8,128)} %copy-done.2, f32[]{:T(128)S(6)} %div.6, f32[1,512,2048]{2,1,0:T(8,128)} %param.6), kind=kLoop, calls=%fused_computation.54 | loop fusion | flops 6291456 | bytes 29360136 | tf_op jit(solution)/shard_map/add | solution.py:137
  (70 shorter events, 96.9 us)
Async XLA Ops:
  0.6 440.7 %copy-start = (f32[8,8]{1,0:T(8,128)S(1)}, f32[8,8]{1,0:T(8,128)}, u32[]{:S(2)}) copy-start(f32[8,8]{1,0:T(8,128)} %param.10) | copy-start | bytes 772
  0.6 93.9 %collective-permute-start.1 = (f32[512,2048]{1,0:T(8,128)}, f32[512,2048]{1,0:T(8,128)}, u32[]{:S(2)}, u32[]{:S(2)}) collective-permute-start(f32[512,2048]{1,0:T(8,128)} %bitcast.127), channel_id=1, source_target_pairs={{0,2},{1,3},{2,0},{3,1},{4,6},{5,7},{6,4},{7,5},{8,10},{9,11},{10,... | collective-permute-start | bytes 12582920 | tf_op jit(solution)/shard_map/ppermute | solution.py:24
  3.7 134.4 %collective-permute-start = (f32[512,2048]{1,0:T(8,128)}, f32[512,2048]{1,0:T(8,128)}, u32[]{:S(2)}, u32[]{:S(2)}) collective-permute-start(f32[512,2048]{1,0:T(8,128)} %bitcast.128), channel_id=1, source_target_pairs={{0,1},{1,0},{2,3},{3,2},{4,5},{5,4},{6,7},{7,6},{8,9},{9,8},{10,11... | collective-permute-start | bytes 12582920 | tf_op jit(solution)/shard_map/ppermute | solution.py:24
  12.2 429.3 %all-to-all-start = ((f32[1,512,2048]{2,0,1:T(1,128)}), f32[1,512,2048]{2,0,1:T(1,128)}, u32[]{:S(2)}, u32[]{:S(2)}) async-start(f32[1,512,2048]{2,0,1:T(1,128)} %copy.27), calls=%async_computation | async-start | bytes 8388608 | tf_op jit(solution)/shard_map/all_to_all | solution.py:115
  94.6 76.5 %collective-permute-start.2 = (f32[512,2048]{1,0:T(8,128)}, f32[512,2048]{1,0:T(8,128)}, u32[]{:S(2)}, u32[]{:S(2)}) collective-permute-start(f32[512,2048]{1,0:T(8,128)} %collective-permute-done.1), channel_id=1, source_target_pairs={{0,1},{1,0},{2,3},{3,2},{4,5},{5,4},{6,7},{7,6},{8,9},{9,8},{10,11... | collective-permute-start | bytes 12582920 | tf_op jit(solution)/shard_map/ppermute | solution.py:24
  133.1 5.0 copy-start.1
  133.1 23.5 %slice-start.4 = ((s8[8388608]{0:T(1024)(128)(4,1)}), s8[4194304]{0:T(1024)(128)(4,1)S(1)}, s32[]{:S(2)}) async-start(s8[8388608]{0:T(1024)(128)(4,1)} %bitcast.150), calls=%async_computation.6 | async-start | bytes 8388608
  138.1 18.5 %slice-start.5 = ((s8[8388608]{0:T(1024)(128)(4,1)}), s8[4194304]{0:T(1024)(128)(4,1)S(1)}, s32[]{:S(2)}) async-start(s8[8388608]{0:T(1024)(128)(4,1)} %bitcast.150), calls=%async_computation.7 | async-start | bytes 8388608
  138.1 37.7 %slice-start.2 = ((s8[8388608]{0:T(1024)(128)(4,1)}), s8[4194304]{0:T(1024)(128)(4,1)S(1)}, s32[]{:S(2)}) async-start(s8[8388608]{0:T(1024)(128)(4,1)} %bitcast.145), calls=%async_computation.4 | async-start | bytes 8388608
  156.6 19.1 %slice-start.3 = ((s8[8388608]{0:T(1024)(128)(4,1)}), s8[4194304]{0:T(1024)(128)(4,1)S(1)}, s32[]{:S(2)}) async-start(s8[8388608]{0:T(1024)(128)(4,1)} %bitcast.145), calls=%async_computation.5 | async-start | bytes 8388608
  436.4 4.5 copy-start.3
  436.4 5.0 copy-start.5
  440.9 67.6 %collective-permute-start.4 = (f32[512,2048]{1,0:T(8,128)}, f32[512,2048]{1,0:T(8,128)}, u32[]{:S(2)}, u32[]{:S(2)}) collective-permute-start(f32[512,2048]{1,0:T(8,128)} %slice.45), channel_id=1, source_target_pairs={{0,1},{1,0},{2,3},{3,2},{4,5},{5,4},{6,7},{7,6},{8,9},{9,8},{10,11... | collective-permute-start | bytes 12582920 | tf_op jit(solution)/shard_map/ppermute | solution.py:24
  462.8 99.5 %all-to-all-start.1 = ((f32[8,64,2048]{2,1,0:T(8,128)}), f32[8,64,2048]{2,1,0:T(8,128)}, u32[]{:S(2)}, u32[]{:S(2)}) async-start(f32[8,64,2048]{2,1,0:T(8,128)} %copy.31), calls=%async_computation.1 | async-start | bytes 8388608 | tf_op jit(solution)/shard_map/all_to_all | solution.py:122
  468.8 39.7 %slice-start = ((s8[8388608]{0:T(1024)(128)(4,1)}), s8[4194304]{0:T(1024)(128)(4,1)S(1)}, s32[]{:S(2)}) async-start(s8[8388608]{0:T(1024)(128)(4,1)} %bitcast.140), calls=%async_computation.2 | async-start | bytes 8388608
  487.2 21.3 %slice-start.1 = ((s8[8388608]{0:T(1024)(128)(4,1)}), s8[4194304]{0:T(1024)(128)(4,1)S(1)}, s32[]{:S(2)}) async-start(s8[8388608]{0:T(1024)(128)(4,1)} %bitcast.140), calls=%async_computation.3 | async-start | bytes 8388608
  505.2 3.2 copy-start.4
  508.5 7.3 %collective-permute-start.3 = (f32[512,2048]{1,0:T(8,128)S(1)}, f32[512,2048]{1,0:T(8,128)}, u32[]{:S(2)}, u32[]{:S(2)}) collective-permute-start(f32[512,2048]{1,0:T(8,128)S(1)} %slice.41), channel_id=1, source_target_pairs={{0,1},{1,0},{2,3},{3,2},{4,5},{5,4},{6,7},{7,6},{8,9},{9,8},{10,11... | collective-permute-start | bytes 12582920 | tf_op jit(solution)/shard_map/ppermute | solution.py:24
  513.6 93.3 %collective-permute-start.5 = (f32[512,2048]{1,0:T(8,128)}, f32[512,2048]{1,0:T(8,128)}, u32[]{:S(2)}, u32[]{:S(2)}) collective-permute-start(f32[512,2048]{1,0:T(8,128)} %slice_add_fusion), channel_id=1, source_target_pairs={{0,2},{1,3},{2,0},{3,1},{4,6},{5,7},{6,4},{7,5},{8,10},{9,11},{10,... | collective-permute-start | bytes 12582920 | tf_op jit(solution)/shard_map/ppermute | solution.py:24
  617.2 2.0 copy-start.2
where the time goes:
time: 687 us; the launch traced here: 682 us
  matrix products  299 us (44%)
  waiting for transfers between devices  159 us (23%)
  local copies, waits for them, and re-layouts  90.7 us (13%)
  other arithmetic  69.8 us (10%)
  blocking collectives  40.9 us (6%)
  starting transfers between devices  17.2 us (3%)
    ppermute x6, waiting for transfers between devices, swap_pairs(): return lax.ppermute(array, 'facet', pairs)  112 us
    dot_general x4, matrix products, body(): jnp.dot(part, table, precision=HIGH)  68.4 us
    dot_general x1, matrix products, row_spectrum_pass(): freqs = jnp.einsum('kpnc,pqknj->kqjc', section, second, precision=HIGH)  47.3 us
    all_to_all x1, waiting for transfers between devices, body(): lax.all_to_all(local_prior, 'chan', split_axis=0, concat_axis=1, tiled=True)  46.5 us
    psum x1, blocking collectives, body(): norm_now, curvature, cross, square = lax.psum(moments, ('chan', 'facet'))  40.9 us
    dot_general x1, matrix products, row_spectrum_pass(): rows = jnp.einsum('kpnc,pqjk->qjnc', section, last, precision=HIGH)  40.1 us
    dot_general x2, matrix products, partial(): lax.dot_general(part[0], table_real, wide, precision=HIGH)  36 us
    dot_general x2, matrix products, partial(): lax.dot_general(part[1], table_imag, wide, precision=HIGH)  35.1 us
  transfers between devices with their start and end apart: 8, of which 4 were waited for; matrix products, arithmetic and copies ran while one was open for 62% of the time, Pallas kernels for 0%

commit v1 on v0

--- a/solution.py
+++ b/solution.py
@@ -119,7 +119,15 @@
     local_prior = PRIOR_FLOOR * regrouped + jnp.einsum(
         "cq,qij->cij", loadings, coeffs, precision=HIGHEST
     )
-    prior_term = lax.all_to_all(local_prior, "chan", split_axis=0, concat_axis=1, tiled=True)
+    ways, here = (lax.axis_size("chan"), lax.axis_index("chan"))
+    width_2 = local_prior.shape[0] // ways
+    turned = jnp.roll(local_prior, -here * width_2, axis=0)
+    got = [lax.slice_in_dim(turned, 0, width_2, axis=0)]
+    for far_2 in range(1, ways):
+        sent = lax.slice_in_dim(turned, far_2 * width_2, (far_2 + 1) * width_2, axis=0)
+        got.append(lax.ppermute(sent, "chan", [(d, (d + far_2) % ways) for d in range(ways)]))
+    line = jnp.concatenate(got[::-1], axis=1)
+    prior_term = jnp.roll(line, (here + 1) * got[0].shape[1], axis=1)
     applied = blurred + prior_term
     moments = jnp.stack(
         [

time: 687 us -> 657 us (0.956)
  waiting for transfers between devices: 159 us -> 123 us
  other arithmetic: 69.8 us -> 61.1 us
  starting transfers between devices: 17.2 us -> 25.1 us
  matrix products: 299 us -> 306 us
    ppermute x0 -> x7, waiting for transfers between devices: none -> 47.9 us  [body(): lax.ppermute(sent, 'chan', [(d, (d + far_2) % ways) for d in range(ways)])]
    all_to_all x1 -> x0, waiting for transfers between devices: 46.5 us -> none  [body(): lax.all_to_all(local_prior, 'chan', split_axis=0, concat_axis=1, tiled=True)]
    ppermute x6, waiting for transfers between devices: 112 us -> 74.8 us  [swap_pairs(): return lax.ppermute(array, 'facet', pairs)]
    ppermute x0 -> x7, starting transfers between devices: none -> 13.8 us  [body(): lax.ppermute(sent, 'chan', [(d, (d + far_2) % ways) for d in range(ways)])]
    unnamed x27 -> x68, local copies, waits for them, and re-layouts: 24.7 us -> 25.6 us
  transfers between devices with their start and end apart: 8 -> 14, of which waited for: 4 -> 4; matrix products, arithmetic and copies ran while one was open for 62% -> 25% of each run, Pallas kernels for 0% -> 0%
where the time goes in v1:
time: 657 us; the launch traced here: 652 us
  matrix products  306 us (47%)
  waiting for transfers between devices  123 us (19%)
  local copies, waits for them, and re-layouts  93.5 us (14%)
  other arithmetic  61.1 us (9%)
  blocking collectives  38.2 us (6%)
  starting transfers between devices  25.1 us (4%)
    ppermute x6, waiting for transfers between devices, swap_pairs(): return lax.ppermute(array, 'facet', pairs)  74.8 us
    dot_general x4, matrix products, body(): jnp.dot(part, table, precision=HIGH)  72 us
    ppermute x7, waiting for transfers between devices, body(): lax.ppermute(sent, 'chan', [(d, (d + far_2) % ways) for d in range(ways)])  47.9 us
    dot_general x1, matrix products, row_spectrum_pass(): freqs = jnp.einsum('kpnc,pqknj->kqjc', section, second, precision=HIGH)  47.4 us
    dot_general x1, matrix products, row_spectrum_pass(): rows = jnp.einsum('kpnc,pqjk->qjnc', section, last, precision=HIGH)  40.1 us
    dot_general x2, matrix products, partial(): lax.dot_general(part[0], table_real, wide, precision=HIGH)  38.2 us
    psum x1, blocking collectives, body(): norm_now, curvature, cross, square = lax.psum(moments, ('chan', 'facet'))  38.2 us
    dot_general x2, matrix products, partial(): lax.dot_general(part[1], table_imag, wide, precision=HIGH)  36.5 us
  transfers between devices with their start and end apart: 14, of which 4 were waited for; matrix products, arithmetic and copies ran while one was open for 25% of the time, Pallas kernels for 0%

profile of v1, /device:TPU:0, one launch (start us, length us, event | category | flops | bytes accessed | tf_op | source)
XLA Modules:
  0.0 651.9 jit_solution(10965610321289318407)
XLA Ops:
  3.7 8.5 %copy.41 = f32[1,512,2048]{2,0,1:T(1,128)} copy(f32[1,512,2048]{2,1,0:T(8,128)} %param.8) | data formatting | bytes 8388608 | tf_op args[2]
  27.5 17.7 %copy.89 = f32[64,64,1024]{2,0,1:T(8,128)} copy(f32[64,64,1024]{2,1,0:T(8,128)} %bitcast.123) | data formatting | bytes 33554432 | tf_op jit(solution)/shard_map/reshape;squeeze | solution.py:54
  45.5 8.3 %fusion.42 = (f32[1,64,64,64]{2,3,0,1:T(8,128)S(1)}, f32[1,64,64,64]{2,3,0,1:T(8,128)S(1)}, f32[1,64,64,64]{2,3,0,1:T(8,128)S(1)}, f32[1,64,64,64]{2,3,0,1:T(8,128)S(1)}, f32[1,64,64,64]{2,3,0,1:T(8,128)S(1)}) fusion(s32[64,64]{0,1:T(8,128)S(1)} %broadcast_multiply_fusion.1, s32[64,64]{1,0:T(8,128)S(1)} %copy.30), kind=kLoop, calls=%fused_computation.75 | loop fusion | flops 4456448 | bytes 5275648 | tf_op jit(solution)/shard_map/sin | solution.py:15
  53.8 40.8 %collective-permute-done.1 = f32[512,2048]{1,0:T(8,128)} collective-permute-done((f32[512,2048]{1,0:T(8,128)}, f32[512,2048]{1,0:T(8,128)}, u32[]{:S(2)}, u32[]{:S(2)}) %collective-permute-start.1) | collective-permute-done | bytes 4194336 | tf_op jit(solution)/shard_map/ppermute | solution.py:24
  106.6 18.2 %fusion.18 = f32[1024,1024]{1,0:T(8,128)} fusion(f32[2048,1024]{1,0:T(8,128)S(1)} %bitcast.132, f32[512,2048]{1,0:T(8,128)} %collective-permute-done, f32[512,2048]{1,0:T(8,128)S(1)} %bitcast.119), kind=kOutput, calls=%fused_computation.28 | convolution fusion | flops 12886999040 | bytes 20971520 | tf_op jit(solution)/shard_map/dot_general | solution.py:85
  124.8 18.0 %fusion.17 = f32[1024,1024]{1,0:T(8,128)} fusion(f32[2048,1024]{1,0:T(8,128)S(1)} %bitcast.140, f32[512,2048]{1,0:T(8,128)} %collective-permute-done, f32[512,2048]{1,0:T(8,128)S(1)} %bitcast.120), kind=kOutput, calls=%fused_computation.27 | convolution fusion | flops 12886999040 | bytes 20971520 | tf_op jit(solution)/shard_map/dot_general | solution.py:85
  163.3 17.8 %fusion.82 = f32[1024,1024]{1,0:T(8,128)} fusion(f32[1024,2048]{1,0:T(8,128)} %constant_dynamic-update-slice_fusion, f32[2048,1024]{1,0:T(8,128)S(1)} %bitcast.135), kind=kOutput, calls=%fused_computation.160 | convolution fusion | flops 12884901888 | bytes 20971520 | tf_op jit(solution)/shard_map/dot_general | solution.py:85
  181.0 18.1 %fusion.83 = f32[1024,1024]{1,0:T(8,128)} fusion(f32[1024,2048]{1,0:T(8,128)} %constant_dynamic-update-slice_fusion, f32[2048,1024]{1,0:T(8,128)S(1)} %bitcast.143), kind=kOutput, calls=%fused_computation.161 | convolution fusion | flops 12884901888 | bytes 20971520 | tf_op jit(solution)/shard_map/dot_general | solution.py:85
  202.4 8.1 %copy.32 = f32[1,32,64,1024]{3,1,0,2:T(8,128)} copy(f32[1,32,64,1024]{3,2,1,0:T(8,128)S(1)} %bitcast.121) | data formatting | bytes 16777216 | tf_op jit(solution)/shard_map/stack | solution.py:82
  214.3 8.1 %copy.33 = f32[1,32,64,1024]{3,1,0,2:T(8,128)} copy(f32[1,32,64,1024]{3,2,1,0:T(8,128)S(1)} %bitcast.122) | data formatting | bytes 16777216 | tf_op jit(solution)/shard_map/stack | solution.py:82
  222.4 27.8 %convolution_bitcast_fusion = f32[64,2,64,1024,1]{3,0,2,1,4:T(8,128)} fusion(f32[1,32,64,1024]{3,1,0,2:T(8,128)} %copy.33, f32[1,32,64,1024]{3,1,0,2:T(8,128)} %copy.32, f32[1,2,32,64]{3,2,0,1:T(8,128)S(1)} %get-tuple-element.34, f32[1,2,32,64]{3,2,0,1:T(8,128)S(1)} %get-tuple-element.35), kind=kOutput, calls=%fused_computation.9 | convolution fusion | flops 3225427968 | bytes 50364416 | tf_op jit(solution)/shard_map/pjnc,pqjk->kqnc/dot_general | solution.py:47
  250.2 47.4 %fusion.6 = f32[64,2,64,1024,1]{3,2,0,1,4:T(8,128)} fusion(f32[64,2,64,1024,1]{3,0,2,1,4:T(8,128)} %convolution_bitcast_fusion, f32[1,2,64,64,64]{3,4,1,2,0:T(8,128)} %get-tuple-element.23, f32[1,2,64,64,64]{3,4,1,2,0:T(8,128)} %get-tuple-element.24), kind=kOutput, calls=%fused_computation.7 | convolution fusion | flops 6443499520 | bytes 71303168 | tf_op jit(solution)/shard_map/kpnc,pqknj->kqjc/dot_general | solution.py:53
  297.7 32.3 %fusion.10 = f32[64,2,64,1024]{3,2,1,0:T(8,128)} fusion(f32[1,2,64,64,64]{3,4,1,2,0:T(8,128)} %get-tuple-element.25, f32[1,2,64,64,64]{3,4,1,2,0:T(8,128)} %get-tuple-element.22, f32[64,2,64,1024,1]{3,2,0,1,4:T(8,128)} %fusion.6, f32[64,64,1024]{2,1,0:T(8,128)} %bitcast.114), kind=kOutput, calls=%fused_computation.14 | convolution fusion | flops 6451888128 | bytes 88080384 | tf_op jit(solution)/shard_map/kpjc,pqknj->kqnc/dot_general | solution.py:57
  329.9 40.1 %fusion.19 = f32[2,32,64,1024]{3,1,2,0:T(8,128)S(1)} fusion(f32[64,2,64,1024]{3,2,1,0:T(8,128)} %fusion.10, f32[1,2,32,64]{3,2,1,0:T(8,128)S(1)} %get-tuple-element.36, f32[1,2,32,64]{3,2,1,0:T(8,128)S(1)} %get-tuple-element.33), kind=kOutput, calls=%fused_computation.29 | convolution fusion | flops 3221233664 | bytes 50364416 | tf_op jit(solution)/shard_map/kpnc,pqjk->qjnc/dot_general | solution.py:59
  370.1 19.4 %copy.40 = f32[2,32,64,1024]{3,2,1,0:T(8,128)} copy(f32[2,32,64,1024]{3,1,2,0:T(8,128)S(1)} %fusion.19) | data formatting | bytes 33554432 | tf_op jit(solution)/shard_map/kpnc,pqjk->qjnc/dot_general | solution.py:59
  389.4 18.1 %fusion.27 = f32[1024,2048]{1,0:T(8,128)} fusion(f32[2048,1024]{1,0:T(8,128)} %bitcast.136, f32[2,2048,1024]{2,1,0:T(8,128)} %bitcast.124), kind=kOutput, calls=%fused_computation.41 | convolution fusion | flops 12884901888 | bytes 20971520 | tf_op jit(solution)/shard_map/dot_general | solution.py:96
  407.6 17.9 %fusion.38 = f32[1024,2048]{1,0:T(8,128)S(1)} fusion(f32[1024,2048]{1,0:T(8,128)} %fusion.27, f32[2048,1024]{1,0:T(8,128)} %bitcast.128, f32[2,2048,1024]{2,1,0:T(8,128)} %bitcast.125), kind=kOutput, calls=%fused_computation.67 | convolution fusion | flops 12886999040 | bytes 29360128 | tf_op jit(solution)/shard_map/dot_general | solution.py:96
  444.3 18.3 %fusion.33 = f32[1024,2048]{1,0:T(8,128)} fusion(f32[2048,1024]{1,0:T(8,128)} %bitcast.137, f32[2,2048,1024]{2,1,0:T(8,128)} %bitcast.126), kind=kOutput, calls=%fused_computation.50 | convolution fusion | flops 12884901888 | bytes 20971520 | tf_op jit(solution)/shard_map/dot_general | solution.py:96
  462.7 20.2 %fusion.37 = f32[1024,2048]{1,0:T(8,128)} fusion(f32[1024,2048]{1,0:T(8,128)} %fusion.33, f32[2048,1024]{1,0:T(8,128)} %bitcast.129, f32[2,2048,1024]{2,1,0:T(8,128)} %bitcast.127), kind=kOutput, calls=%fused_computation.66 | convolution fusion | flops 12886999040 | bytes 29360128 | tf_op jit(solution)/shard_map/dot_general | solution.py:96
  499.7 31.8 %collective-permute-done.9 = f32[1,64,2048]{2,1,0:T(8,128)S(1)} collective-permute-done((f32[1,64,2048]{2,1,0:T(8,128)}, f32[1,64,2048]{2,1,0:T(8,128)S(1)}, u32[]{:S(2)}, u32[]{:S(2)}) %collective-permute-start.9) | collective-permute-done | bytes 524320 | tf_op jit(solution)/shard_map/ppermute | solution.py:128
  531.9 16.0 %collective-permute-done.12 = f32[1,64,2048]{2,1,0:T(8,128)S(1)} collective-permute-done((f32[1,64,2048]{2,1,0:T(8,128)S(1)}, f32[1,64,2048]{2,1,0:T(8,128)S(1)}, u32[]{:S(2)}, u32[]{:S(2)}) %collective-permute-start.12) | collective-permute-done | bytes 524320 | tf_op jit(solution)/shard_map/ppermute | solution.py:128
  551.6 34.1 %collective-permute-done.5 = f32[512,2048]{1,0:T(8,128)} collective-permute-done((f32[512,2048]{1,0:T(8,128)S(1)}, f32[512,2048]{1,0:T(8,128)}, u32[]{:S(2)}, u32[]{:S(2)}) %collective-permute-start.5) | collective-permute-done | bytes 4194336 | tf_op jit(solution)/shard_map/ppermute | solution.py:24
  596.0 38.2 %psum.7 = f32[4]{0:T(128)S(1)} all-reduce(f32[4]{0:T(128)S(1)} %pad_maximum_fusion.14), channel_id=1, replica_groups=mesh['chan'=8,'facet'=4] {'chan','facet'}, use_global_device_ids=true, to_apply=%region_4.5 | all-reduce | flops 4 | bytes 32 | tf_op jit(solution)/shard_map/psum | solution.py:140
  638.6 12.8 %multiply_add_fusion.1 = (f32[1,512,2048]{2,1,0:T(8,128)}, f32[1,512,2048]{2,1,0:T(8,128)}, f32[1,512,2048]{2,1,0:T(8,128)}) fusion(f32[1,512,2048]{2,1,0:T(8,128)} %param.8, f32[]{:T(128)S(6)} %div.7, f32[1,512,2048]{2,1,0:T(8,128)} %param.7, f32[1,512,2048]{2,1,0:T(8,128)} %get-tuple-element.13, f32[]{:T(128)S(6)} %div.6, f32[1,512,2048]{2,1,0:T(8,128)} %param.6), kind=kLoop, calls=%fused_computation.56 | loop fusion | flops 6291456 | bytes 29360136 | tf_op jit(solution)/shard_map/add | solution.py:145
  (126 shorter events, 108.3 us)
Async XLA Ops:
  0.6 44.7 %copy-start = (f32[8,8]{1,0:T(8,128)S(1)}, f32[8,8]{1,0:T(8,128)}, u32[]{:S(2)}) copy-start(f32[8,8]{1,0:T(8,128)} %param.10) | copy-start | bytes 772
  0.6 93.9 %collective-permute-start.1 = (f32[512,2048]{1,0:T(8,128)}, f32[512,2048]{1,0:T(8,128)}, u32[]{:S(2)}, u32[]{:S(2)}) collective-permute-start(f32[512,2048]{1,0:T(8,128)} %bitcast.117), channel_id=1, source_target_pairs={{0,2},{1,3},{2,0},{3,1},{4,6},{5,7},{6,4},{7,5},{8,10},{9,11},{10,... | collective-permute-start | bytes 12582920 | tf_op jit(solution)/shard_map/ppermute | solution.py:24
  12.2 130.5 %all-to-all-start = ((f32[1,512,2048]{2,0,1:T(1,128)}), f32[1,512,2048]{2,0,1:T(1,128)}, u32[]{:S(2)}, u32[]{:S(2)}) async-start(f32[1,512,2048]{2,0,1:T(1,128)} %copy.41), calls=%async_computation | async-start | bytes 8388608 | tf_op jit(solution)/shard_map/all_to_all | solution.py:115
  18.3 88.2 %collective-permute-start = (f32[512,2048]{1,0:T(8,128)}, f32[512,2048]{1,0:T(8,128)}, u32[]{:S(2)}, u32[]{:S(2)}) collective-permute-start(f32[512,2048]{1,0:T(8,128)} %bitcast.118), channel_id=1, source_target_pairs={{0,1},{1,0},{2,3},{3,2},{4,5},{5,4},{6,7},{7,6},{8,9},{9,8},{10,11... | collective-permute-start | bytes 12582920 | tf_op jit(solution)/shard_map/ppermute | solution.py:24
  45.5 61.0 %slice-start = ((s8[8388608]{0:T(1024)(128)(4,1)}), s8[4194304]{0:T(1024)(128)(4,1)S(1)}, s32[]{:S(2)}) async-start(s8[8388608]{0:T(1024)(128)(4,1)} %bitcast.130), calls=%async_computation.1 | async-start | bytes 8388608
  94.6 63.8 %collective-permute-start.2 = (f32[512,2048]{1,0:T(8,128)}, f32[512,2048]{1,0:T(8,128)}, u32[]{:S(2)}, u32[]{:S(2)}) collective-permute-start(f32[512,2048]{1,0:T(8,128)} %collective-permute-done.1), channel_id=1, source_target_pairs={{0,1},{1,0},{2,3},{3,2},{4,5},{5,4},{6,7},{7,6},{8,9},{9,8},{10,11... | collective-permute-start | bytes 12582920 | tf_op jit(solution)/shard_map/ppermute | solution.py:24
  101.5 23.2 %slice-start.4 = ((s8[8388608]{0:T(1024)(128)(4,1)}), s8[4194304]{0:T(1024)(128)(4,1)S(1)}, s32[]{:S(2)}) async-start(s8[8388608]{0:T(1024)(128)(4,1)} %bitcast.138), calls=%async_computation.5 | async-start | bytes 8388608
  106.5 18.2 %slice-start.5 = ((s8[8388608]{0:T(1024)(128)(4,1)}), s8[4194304]{0:T(1024)(128)(4,1)S(1)}, s32[]{:S(2)}) async-start(s8[8388608]{0:T(1024)(128)(4,1)} %bitcast.138), calls=%async_computation.6 | async-start | bytes 8388608
  158.4 22.6 %slice-start.6 = ((s8[8388608]{0:T(1024)(128)(4,1)}), s8[4194304]{0:T(1024)(128)(4,1)S(1)}, s32[]{:S(2)}) async-start(s8[8388608]{0:T(1024)(128)(4,1)} %bitcast.141), calls=%async_computation.7 | async-start | bytes 8388608
  181.0 18.1 %copy-start.10 = (f32[1024,1024]{1,0:T(8,128)S(1)}, f32[1024,1024]{1,0:T(8,128)}, u32[]{:S(2)}) copy-start(f32[1024,1024]{1,0:T(8,128)} %fusion.18) | copy-start | bytes 12582916
  427.9 59.7 %collective-permute-start.4 = (f32[512,2048]{1,0:T(8,128)}, f32[512,2048]{1,0:T(8,128)S(1)}, u32[]{:S(2)}, u32[]{:S(2)}) collective-permute-start(f32[512,2048]{1,0:T(8,128)} %slice.77), channel_id=1, source_target_pairs={{0,1},{1,0},{2,3},{3,2},{4,5},{5,4},{6,7},{7,6},{8,9},{9,8},{10,11... | collective-permute-start | bytes 12582920 | tf_op jit(solution)/shard_map/ppermute | solution.py:24
  436.1 56.4 %collective-permute-start.6 = (f32[1,64,2048]{2,1,0:T(8,128)}, f32[1,64,2048]{2,1,0:T(8,128)S(1)}, u32[]{:S(2)}, u32[]{:S(2)}) collective-permute-start(f32[1,64,2048]{2,1,0:T(8,128)} %get-tuple-element.21), channel_id=1, source_target_pairs={{0,28},{4,0},{8,4},{12,8},{16,12},{20,16},{24,20},{28,24},{1,29},{... | collective-permute-start | bytes 1572872 | tf_op jit(solution)/shard_map/ppermute | solution.py:128
  440.9 53.2 %collective-permute-start.7 = (f32[1,64,2048]{2,1,0:T(8,128)}, f32[1,64,2048]{2,1,0:T(8,128)S(1)}, u32[]{:S(2)}, u32[]{:S(2)}) collective-permute-start(f32[1,64,2048]{2,1,0:T(8,128)} %get-tuple-element.20), channel_id=1, source_target_pairs={{0,24},{4,28},{8,0},{12,4},{16,8},{20,12},{24,16},{28,20},{1,25},{... | collective-permute-start | bytes 1572872 | tf_op jit(solution)/shard_map/ppermute | solution.py:128
  441.4 52.9 %collective-permute-start.8 = (f32[1,64,2048]{2,1,0:T(8,128)}, f32[1,64,2048]{2,1,0:T(8,128)S(1)}, u32[]{:S(2)}, u32[]{:S(2)}) collective-permute-start(f32[1,64,2048]{2,1,0:T(8,128)} %get-tuple-element.19), channel_id=1, source_target_pairs={{0,20},{4,24},{8,28},{12,0},{16,4},{20,8},{24,12},{28,16},{1,21},{... | collective-permute-start | bytes 1572872 | tf_op jit(solution)/shard_map/ppermute | solution.py:128
  441.4 90.1 %collective-permute-start.9 = (f32[1,64,2048]{2,1,0:T(8,128)}, f32[1,64,2048]{2,1,0:T(8,128)S(1)}, u32[]{:S(2)}, u32[]{:S(2)}) collective-permute-start(f32[1,64,2048]{2,1,0:T(8,128)} %get-tuple-element.18), channel_id=1, source_target_pairs={{0,16},{4,20},{8,24},{12,28},{16,0},{20,4},{24,8},{28,12},{1,17},{... | collective-permute-start | bytes 1572872 | tf_op jit(solution)/shard_map/ppermute | solution.py:128
  489.6 62.0 %collective-permute-start.3 = (f32[512,2048]{1,0:T(8,128)}, f32[512,2048]{1,0:T(8,128)}, u32[]{:S(2)}, u32[]{:S(2)}) collective-permute-start(f32[512,2048]{1,0:T(8,128)} %slice.73), channel_id=1, source_target_pairs={{0,1},{1,0},{2,3},{3,2},{4,5},{5,4},{6,7},{7,6},{8,9},{9,8},{10,11... | collective-permute-start | bytes 12582920 | tf_op jit(solution)/shard_map/ppermute | solution.py:24
  489.6 96.0 %slice-start.8 = ((s8[8388608]{0:T(1024)(128)(4,1)}), s8[4194304]{0:T(1024)(128)(4,1)S(1)}, s32[]{:S(2)}) async-start(s8[8388608]{0:T(1024)(128)(4,1)} %bitcast.144), calls=%async_computation.9 | async-start | bytes 8388608
  492.5 93.2 %copy-start.5 = (f32[1,512,2048]{2,1,0:T(8,128)S(1)}, f32[1,512,2048]{2,1,0:T(8,128)}, u32[]{:S(2)}) copy-start(f32[1,512,2048]{2,1,0:T(8,128)} %param.8) | copy-start | bytes 12582916
  492.5 93.2 %copy-start.7 = (f32[1,512,2048]{2,1,0:T(8,128)S(1)}, f32[1,512,2048]{2,1,0:T(8,128)}, u32[]{:S(2)}) copy-start(f32[1,512,2048]{2,1,0:T(8,128)} %param.7) | copy-start | bytes 12582916
  492.5 93.2 %collective-permute-start.5 = (f32[512,2048]{1,0:T(8,128)S(1)}, f32[512,2048]{1,0:T(8,128)}, u32[]{:S(2)}, u32[]{:S(2)}) collective-permute-start(f32[512,2048]{1,0:T(8,128)S(1)} %slice_add_fusion), channel_id=1, source_target_pairs={{0,2},{1,3},{2,0},{3,1},{4,6},{5,7},{6,4},{7,5},{8,10},{9,11},{10,... | collective-permute-start | bytes 12582920 | tf_op jit(solution)/shard_map/ppermute | solution.py:24
  494.2 37.6 %collective-permute-start.10 = (f32[1,64,2048]{2,1,0:T(8,128)S(1)}, f32[1,64,2048]{2,1,0:T(8,128)S(1)}, u32[]{:S(2)}, u32[]{:S(2)}) collective-permute-start(f32[1,64,2048]{2,1,0:T(8,128)S(1)} %copy-done.13), channel_id=1, source_target_pairs={{0,12},{4,16},{8,20},{12,24},{16,28},{20,0},{24,4},{28,8},{1,13},{... | collective-permute-start | bytes 1572872 | tf_op jit(solution)/shard_map/ppermute | solution.py:128
  494.3 91.4 %slice-start.9 = ((s8[8388608]{0:T(1024)(128)(4,1)}), s8[4194304]{0:T(1024)(128)(4,1)S(1)}, s32[]{:S(2)}) async-start(s8[8388608]{0:T(1024)(128)(4,1)} %bitcast.144), calls=%async_computation.10 | async-start | bytes 8388608
  494.3 37.6 %collective-permute-start.11 = (f32[1,64,2048]{2,1,0:T(8,128)S(1)}, f32[1,64,2048]{2,1,0:T(8,128)S(1)}, u32[]{:S(2)}, u32[]{:S(2)}) collective-permute-start(f32[1,64,2048]{2,1,0:T(8,128)S(1)} %copy-done.12), channel_id=1, source_target_pairs={{0,8},{4,12},{8,16},{12,20},{16,24},{20,28},{24,0},{28,4},{1,9},{5... | collective-permute-start | bytes 1572872 | tf_op jit(solution)/shard_map/ppermute | solution.py:128
  531.5 16.4 %collective-permute-start.12 = (f32[1,64,2048]{2,1,0:T(8,128)S(1)}, f32[1,64,2048]{2,1,0:T(8,128)S(1)}, u32[]{:S(2)}, u32[]{:S(2)}) collective-permute-start(f32[1,64,2048]{2,1,0:T(8,128)S(1)} %get-tuple-element.15), channel_id=1, source_target_pairs={{0,4},{4,8},{8,12},{12,16},{16,20},{20,24},{24,28},{28,0},{1,5},{5... | collective-permute-start | bytes 1572872 | tf_op jit(solution)/shard_map/ppermute | solution.py:128
  (15 other events, 138.3 us)
